TPU v7x, 256 devices: a whole 4x4x8 slice. The times are simulated.
256 devices in a mesh: dp: 16 (over y_lo, x, core), ctx: 16 (over y_hi, z).
Axes of the slice: x: 4, y: 4 (y_hi: 2, y_lo: 2; y = y_hi * 2 + y_lo), z: 8, core: 2. Of those that a mesh axis runs over, the one named last changes fastest.
Arguments:
- roll_query: bfloat16 [16, 2048, 4096], P('dp', 'ctx'), may hold values from -12 to 12
- roll_keys: bfloat16 [16, 2048, 512], P('dp', 'ctx'), may hold values from -12 to 12
- roll_values: bfloat16 [16, 2048, 512], P('dp', 'ctx'), may hold values from -6 to 6
- pack_dest: int32 [16, 256], P(None, 'ctx'), may hold values from 0 to 15, as said below
- segment_ids: int32 [16, 2048], P('dp', 'ctx'), may hold values from 0 to 15, never falling along the last dimension, each value on 1 to 1024 neighbouring positions
- reward_bins: int32 [16, 16], P('dp'), may hold values from 0 to 511
- reward_weight: float32 [4096], replicated, may hold values from -0.5 to 0.5
Outputs:
- attention_out: bfloat16 [16, 2048, 4096], P('dp', 'ctx')
- reward_hist: float32 [512], replicated
Inputs may be any that keep to these rules, and one draw needn't show every extreme that they name: For every column j the entries pack_dest[s, j] over s are a permutation of the packed sequences. Among the 16 columns of one ctx shard, at most 1 block go from one source to one packed sequence, and exactly 1 for some pair in every shard.
All inputs are finite; a program needn't handle non-finite values.
Results may differ from a plain program's by a relative error of at most 0.004.
Values may be sent and summed in bfloat16 or wider, within the bound.
A program may use at most 64 MiB of HBM per device.

v0:
```python
import math
import jax
import jax.numpy as jnp
from jax import lax
from jax.sharding import PartitionSpec as P

HQ = 32
HK = 4
HD = 128
BLK = 8
SEGS = 16
BINS = 512
NEG = -1e30


def shifted(block, axis, distance):
    devices = range(lax.axis_size(axis))
    route = [(i - distance, i) for i in devices if i - distance in devices]
    return lax.ppermute(block, axis, route)


def block_rank(labels):
    count_all = labels.shape[0]
    earlier = jnp.arange(count_all)[:, None] < jnp.arange(count_all)[None, :]
    same_label = labels[:, None] == labels[None, :]
    return jnp.sum(jnp.where(same_label & earlier, 1, 0), axis=0).astype(jnp.int32)


def select_rows(selector, source_rows):
    flat_rows = source_rows.reshape(selector.shape[1], -1)
    return jnp.dot(selector, flat_rows, preferred_element_type=jnp.float32).astype(jnp.bfloat16)


def local(roll_query, roll_keys, roll_values, pack_dest, segment_ids, reward_bins, reward_weight):
    dp_count = lax.axis_size("dp")
    dp_self = lax.axis_index("dp")
    ctx_self = lax.axis_index("ctx")
    row_count = roll_query.shape[1]
    block_count = row_count // BLK
    q_width = roll_query.shape[2]
    kv_width = roll_keys.shape[2]
    cap_here = (block_count + dp_count - 1) // dp_count
    slot_count = dp_count * cap_here
    group_size = HQ // HK
    score_scale = 1.0 / math.sqrt(HD)
    own_dest = lax.dynamic_index_in_dim(pack_dest, dp_self, 0, keepdims=False)
    send_slot = own_dest * cap_here + block_rank(own_dest)
    send_sel = (jnp.arange(slot_count, dtype=jnp.int32)[:, None] == send_slot[None, :]).astype(
        jnp.bfloat16
    )
    send_query = select_rows(send_sel, roll_query[0]).reshape(dp_count, cap_here * BLK, q_width)
    send_keys = select_rows(send_sel, roll_keys[0]).reshape(dp_count, cap_here * BLK, kv_width)
    send_values = select_rows(send_sel, roll_values[0]).reshape(dp_count, cap_here * BLK, kv_width)
    got_query, got_keys, got_values = (
        lax.all_to_all(send_query, "dp", split_axis=0, concat_axis=0, tiled=True),
        lax.all_to_all(send_keys, "dp", split_axis=0, concat_axis=0, tiled=True),
        lax.all_to_all(send_values, "dp", split_axis=0, concat_axis=0, tiled=True),
    )
    matched = pack_dest == dp_self
    earlier = jnp.arange(block_count)[:, None] < jnp.arange(block_count)[None, :]
    recv_rank = jnp.sum(jnp.where(matched[:, :, None] & earlier[None], 1, 0), axis=1)
    source_ids = jnp.arange(dp_count, dtype=jnp.int32)[:, None]
    recv_slot = jnp.sum(jnp.where(matched, source_ids * cap_here + recv_rank, 0), axis=0)
    recv_sel = (recv_slot[:, None] == jnp.arange(slot_count, dtype=jnp.int32)[None, :]).astype(
        jnp.bfloat16
    )
    packed_query = select_rows(recv_sel, got_query).reshape(row_count, q_width)
    packed_keys = select_rows(recv_sel, got_keys).reshape(row_count, kv_width)
    packed_values = select_rows(recv_sel, got_values).reshape(row_count, kv_width)
    seg_local = segment_ids[0]
    query_heads = packed_query.reshape(row_count, HK, group_size, HD)
    query_pos = ctx_self * row_count + jnp.arange(row_count, dtype=jnp.int32)

    def attend_block(running, key_rows, value_rows, key_segments, first_row):
        key_count = key_rows.shape[0]
        key_pos = first_row + jnp.arange(key_count, dtype=jnp.int32)
        allowed = (seg_local[:, None] == key_segments[None, :]) & (
            key_pos[None, :] <= query_pos[:, None]
        )
        scores = (
            jnp.einsum(
                "qgjd,kgd->gjqk",
                query_heads,
                key_rows.reshape(key_count, HK, HD),
                preferred_element_type=jnp.float32,
            )
            * score_scale
        )
        scores = jnp.where(allowed, scores, NEG)
        run_max, run_sum, run_acc = running
        new_max = jnp.maximum(run_max, jnp.max(scores, axis=-1))
        weights = jnp.where(allowed, jnp.exp(scores - new_max[..., None]), 0.0)
        shrink = jnp.exp(run_max - new_max)
        new_sum = run_sum * shrink + jnp.sum(weights, axis=-1)
        update = jnp.einsum(
            "gjqk,kgd->qgjd",
            weights.astype(jnp.bfloat16),
            value_rows.reshape(key_count, HK, HD),
            preferred_element_type=jnp.float32,
        )
        new_acc = run_acc * jnp.transpose(shrink, (2, 0, 1))[..., None] + update
        return (new_max, new_sum, new_acc)

    initial = (
        jnp.full((HK, group_size, row_count), NEG, jnp.float32),
        jnp.zeros((HK, group_size, row_count), jnp.float32),
        jnp.zeros((row_count, HK, group_size, HD), jnp.float32),
    )
    key_rows = lax.all_gather(packed_keys, "ctx", axis=0, tiled=True)
    value_rows = lax.all_gather(packed_values, "ctx", axis=0, tiled=True)
    key_segments = lax.all_gather(seg_local, "ctx", axis=0, tiled=True)
    key_count = key_rows.shape[0]

    def sub_block(turn_index, carried):
        offset = turn_index * row_count
        return attend_block(
            carried,
            lax.dynamic_slice_in_dim(key_rows, offset, row_count, 0),
            lax.dynamic_slice_in_dim(value_rows, offset, row_count, 0),
            lax.dynamic_slice_in_dim(key_segments, offset, row_count, 0),
            offset,
        )

    final_max, final_sum, final_acc = lax.fori_loop(0, key_count // row_count, sub_block, initial)
    attended = (
        (final_acc / jnp.transpose(final_sum, (2, 0, 1))[..., None])
        .reshape(row_count, q_width)
        .astype(jnp.bfloat16)
    )
    next_first = shifted(seg_local[:1] + 1, "ctx", -1)
    next_plus = jnp.concatenate([seg_local[1:] + 1, next_first])
    is_end = next_plus != seg_local + 1
    row_reward = jnp.dot(
        attended, reward_weight, precision=lax.Precision.HIGHEST, preferred_element_type=jnp.float32
    )
    kept = jnp.where(is_end, row_reward, 0.0)
    seg_match = seg_local[:, None] == jnp.arange(SEGS, dtype=jnp.int32)[None, :]
    bin_of = jnp.sum(jnp.where(seg_match, reward_bins[0][None, :], 0), axis=1)
    bin_match = bin_of[:, None] == jnp.arange(BINS, dtype=jnp.int32)[None, :]
    local_hist = jnp.sum(jnp.where(bin_match, kept[:, None], 0.0), axis=0)
    histogram = lax.psum(local_hist, ("dp", "ctx"))
    return (attended.reshape(1, row_count, q_width), histogram)


def solution(mesh):
    in_specs = (
        P("dp", "ctx", None),
        P("dp", "ctx", None),
        P("dp", "ctx", None),
        P(None, "ctx"),
        P("dp", "ctx"),
        P("dp", None),
        P(),
    )
    out_specs = (P("dp", "ctx", None), P())
    return jax.shard_map(local, mesh=mesh, in_specs=in_specs, out_specs=out_specs, check_vma=False)
```

profile of v0, /device:TPU:1, one launch (start us, length us, event | category | flops | bytes accessed | tf_op | source)
XLA Modules:
  0.0 377.6 jit_solution(7069641416522338953)
XLA Ops:
  8.7 1.0 reshape_squeeze.9
  10.6 6.8 %all-to-all-start = ((bf16[16,8,512]{2,1,0:T(8,128)(2,1)}), bf16[16,8,512]{2,1,0:T(8,128)(2,1)S(1)}, u32[]{:S(2)}, u32[]{:S(2)}) async-start(bf16[16,8,512]{2,1,0:T(8,128)(2,1)} %bitcast.28), calls=%async_computation | async-start | bytes 262144 | tf_op jit(solution)/shard_map/all_to_all | solution.py:56
  19.0 4.5 %all-to-all-done = bf16[16,8,512]{2,1,0:T(8,128)(2,1)S(1)} async-done(((bf16[16,8,512]{2,1,0:T(8,128)(2,1)}), bf16[16,8,512]{2,1,0:T(8,128)(2,1)S(1)}, u32[]{:S(2)}, u32[]{:S(2)}) %all-to-all-start) | async-done | bytes 131104 | tf_op jit(solution)/shard_map/all_to_all | solution.py:56
  24.9 9.0 %all_to_all.15 = bf16[16,8,512]{2,1,0:T(8,128)(2,1)S(1)} all-to-all(bf16[16,8,512]{2,1,0:T(8,128)(2,1)S(1)} %bitcast.106), channel_id=1, replica_groups=mesh['dp'=16,'ctx'=16] {'dp'}, dimensions={0} | all-to-all | bytes 262144 | tf_op jit(solution)/shard_map/all_to_all | solution.py:57
  34.3 0.8 copy.22
  36.1 1.5 copy.33
  37.7 3.9 %all-to-all-start.1 = ((bf16[16,8,4096]{2,1,0:T(8,128)(2,1)}), bf16[16,8,4096]{2,1,0:T(8,128)(2,1)S(1)}, u32[]{:S(2)}, u32[]{:S(2)}) async-start(bf16[16,8,4096]{2,1,0:T(8,128)(2,1)} %bitcast.32), calls=%async_computation.1 | async-start | bytes 2097152 | tf_op jit(solution)/shard_map/all_to_all | solution.py:55
  41.6 1.3 collective-permute-start
  43.0 38.5 %all-gather = s32[1,2048]{1,0:T(1,128)S(1)} all-gather(s32[1,128]{1,0:T(1,128)S(1)} %copy-done.3), channel_id=2, replica_groups=mesh['dp'=16,'ctx'=16] {'ctx'}, dimensions={1}, use_global_device_ids=true | all-gather | bytes 8704 | tf_op jit(solution)/shard_map/all_gather | solution.py:111
  83.6 23.9 %all-gather.4.cloned.1.call-done = bf16[2048,512]{0,1:T(8,128)(2,1)} async-done(((bf16[128,512]{0,1:T(8,128)(2,1)}), bf16[2048,512]{0,1:T(8,128)(2,1)}) %all-gather.4.cloned.1.call-update) | async-done | bytes 2097168 | tf_op jit(solution)/shard_map/all_gather | solution.py:109
  107.5 84.1 %all-gather.6.cloned.1.call-done = bf16[2048,512]{0,1:T(8,128)(2,1)} async-done(((bf16[128,512]{0,1:T(8,128)(2,1)}), bf16[2048,512]{0,1:T(8,128)(2,1)}) %all-gather.6.cloned.1.call-update) | async-done | bytes 2097168 | tf_op jit(solution)/shard_map/all_gather | solution.py:110
  191.6 96.3 %while.18 = (s32[]{:T(128)}, f32[4,8,128]{2,1,0:T(8,128)S(1)}, f32[4,8,128]{2,1,0:T(8,128)S(1)}, f32[128,4,8,128]{0,3,2,1:T(8,128)}, s32[1,128]{1,0:T(1,128)S(1)...) while((s32[]{:T(128)}, f32[4,8,128]{2,1,0:T(8,128)S(1)}, ...), condition=%wide.region_6.7_spmd.clone, body=%wide.region_3.6_spmd.clone.sunk | while | flops 276898048 | bytes 12652751 | solution.py:124
  191.8 1.0 constant_dynamic-slice_fusion.4
  193.3 2.2 bitcast_add_fusion.3
  196.3 1.0 constant_dynamic-slice_fusion.4
  197.9 3.8 bitcast_add_fusion.3
  202.4 1.0 constant_dynamic-slice_fusion.4
  204.0 3.8 bitcast_add_fusion.3
  208.6 1.0 constant_dynamic-slice_fusion.4
  210.1 3.8 bitcast_add_fusion.3
  214.7 1.0 constant_dynamic-slice_fusion.4
  216.2 3.8 bitcast_add_fusion.3
  220.8 1.0 constant_dynamic-slice_fusion.4
  222.4 3.8 bitcast_add_fusion.3
  226.9 1.0 constant_dynamic-slice_fusion.4
  228.5 3.8 bitcast_add_fusion.3
  233.1 1.0 constant_dynamic-slice_fusion.4
  234.6 3.8 bitcast_add_fusion.3
  239.2 1.0 constant_dynamic-slice_fusion.4
  240.7 3.8 bitcast_add_fusion.3
  245.3 1.0 constant_dynamic-slice_fusion.4
  246.9 3.8 bitcast_add_fusion.3
  251.4 1.0 constant_dynamic-slice_fusion.4
  253.0 3.8 bitcast_add_fusion.3
  257.5 1.0 constant_dynamic-slice_fusion.4
  259.1 3.8 bitcast_add_fusion.3
  263.7 1.0 constant_dynamic-slice_fusion.4
  265.2 3.8 bitcast_add_fusion.3
  269.8 1.0 constant_dynamic-slice_fusion.4
  271.3 3.8 bitcast_add_fusion.3
  275.9 1.0 constant_dynamic-slice_fusion.4
  277.5 3.8 bitcast_add_fusion.3
  282.0 1.0 constant_dynamic-slice_fusion.4
  283.6 3.8 bitcast_add_fusion.3
  287.9 1.9 divide_convert_fusion
  289.8 1.3 copy.28
  291.1 1.1 compare_select_fusion
  292.4 78.4 %psum.7 = f32[512]{0:T(512)} all-reduce(f32[512]{0:T(512)S(1)} %select_reduce_fusion), channel_id=1, replica_groups=mesh['dp'=16,'ctx'=16] {'dp','ctx'}, use_global_device_ids=true, to_apply=%region_9.10 | all-reduce | flops 512 | bytes 4096 | tf_op jit(solution)/shard_map/psum | solution.py:141
  (175 shorter events, 29.7 us)
Async XLA Ops:
  7.2 284.0 %copy-start = (f32[4096]{0:T(1024)S(1)}, f32[4096]{0:T(1024)}, u32[]{:S(2)}) copy-start(f32[4096]{0:T(1024)} %param.15) | copy-start | bytes 49156
  7.2 17.5 %copy-start.2 = (bf16[1,128,512]{2,1,0:T(8,128)(2,1)S(1)}, bf16[1,128,512]{2,1,0:T(8,128)(2,1)}, u32[]{:S(2)}) copy-start(bf16[1,128,512]{2,1,0:T(8,128)(2,1)} %param.11) | copy-start | bytes 393220
  9.7 25.4 %copy-start.1 = (bf16[1,128,4096]{2,1,0:T(8,128)(2,1)S(1)}, bf16[1,128,4096]{2,1,0:T(8,128)(2,1)}, u32[]{:S(2)}) copy-start(bf16[1,128,4096]{2,1,0:T(8,128)(2,1)} %param.9) | copy-start | bytes 3145732
  10.6 12.9 %all-to-all-start = ((bf16[16,8,512]{2,1,0:T(8,128)(2,1)}), bf16[16,8,512]{2,1,0:T(8,128)(2,1)S(1)}, u32[]{:S(2)}, u32[]{:S(2)}) async-start(bf16[16,8,512]{2,1,0:T(8,128)(2,1)} %bitcast.28), calls=%async_computation | async-start | bytes 262144 | tf_op jit(solution)/shard_map/all_to_all | solution.py:56
  17.4 90.1 %all-gather.4.cloned.1.call-start = ((), (), s32[]{:S(2)}) async-start(), calls=%async_computation.3 | async-start | bytes 2228224 | tf_op jit(solution)/shard_map/all_gather | solution.py:109
  24.6 167.0 %all-gather.6.cloned.1.call-start = ((), (), s32[]{:S(2)}) async-start(), calls=%async_computation.4 | async-start | bytes 2228224 | tf_op jit(solution)/shard_map/all_gather | solution.py:110
  36.1 5.5 %copy-start.3 = (s32[1,128]{1,0:T(1,128)S(1)}, s32[1,128]{1,0:T(1,128)}, u32[]{:S(2)}) copy-start(s32[1,128]{1,0:T(1,128)} %param.13) | copy-start | bytes 1540
  36.1 45.3 %copy-start.4 = (s32[1,16]{1,0:T(1,128)S(1)}, s32[1,16]{1,0:T(1,128)}, u32[]{:S(2)}) copy-start(s32[1,16]{1,0:T(1,128)} %param.14) | copy-start | bytes 196
  37.7 43.9 %all-to-all-start.1 = ((bf16[16,8,4096]{2,1,0:T(8,128)(2,1)}), bf16[16,8,4096]{2,1,0:T(8,128)(2,1)S(1)}, u32[]{:S(2)}, u32[]{:S(2)}) async-start(bf16[16,8,4096]{2,1,0:T(8,128)(2,1)} %bitcast.32), calls=%async_computation.1 | async-start | bytes 2097152 | tf_op jit(solution)/shard_map/all_to_all | solution.py:55
  41.6 249.5 %collective-permute-start = (s32[1]{0:T(128)}, s32[1]{0:T(128)}, u32[]{:S(2)}, u32[]{:S(2)}) collective-permute-start(s32[1]{0:T(128)} %bitcast.9), channel_id=1, source_target_pairs={{1,0},{2,1},{3,2},{4,3},{5,4},{6,5},{7,6},{8,7},{9,8},{10,9},{11,1... | collective-permute-start | bytes 20 | tf_op jit(solution)/shard_map/ppermute | solution.py:19
Sparse Core Ops, SparseCore 0:
  24.7 82.7 all-gather.3
  110.0 81.5 all-gather.5
where the time goes:
time: 379 us; the launch traced here: 378 us
  blocking collectives  126 us (33%)
  waiting for transfers between devices  112 us (30%)
  matrix products  69.7 us (18%)
  local copies, waits for them, and re-layouts  26.4 us (7%)
  other arithmetic  15.5 us (4%)
  between operations  14.3 us (4%)
  starting transfers between devices  12.1 us (3%)
    all_gather x1, waiting for transfers between devices, local(): value_rows = lax.all_gather(packed_values, 'ctx', axis=0, tiled=True)  84.1 us
    psum x1, blocking collectives, local(): histogram = lax.psum(local_hist, ('dp', 'ctx'))  78.4 us
    dot_general x16, matrix products, attend_block(): jnp.einsum('gjqk,kgd->qgjd', weights.astype(jnp.bfloat16), value_rows.res...  58.6 us
    all_gather x1, blocking collectives, local(): key_segments = lax.all_gather(seg_local, 'ctx', axis=0, tiled=True)  38.5 us
    all_gather x1, waiting for transfers between devices, local(): key_rows = lax.all_gather(packed_keys, 'ctx', axis=0, tiled=True)  23.9 us
    dynamic_slice x16, local copies, waits for them, and re-layouts, sub_block(): lax.dynamic_slice_in_dim(value_rows, offset, row_count, 0)  16 us
    all_to_all x1, blocking collectives, local(): lax.all_to_all(send_values, 'dp', split_axis=0, concat_axis=0, tiled=True)  9.04 us
    reduce_sum x16, other arithmetic, attend_block(): new_sum = run_sum * shrink + jnp.sum(weights, axis=-1)  8.93 us
  transfers between devices with their start and end apart: 5, of which 3 were waited for; matrix products, arithmetic and copies ran while one was open for 28% of the time, Pallas kernels for 0%

commit v1 on v0

--- a/solution.py
+++ b/solution.py
@@ -11,6 +11,11 @@
 SEGS = 16
 BINS = 512
 NEG = -1e30
+
+
+def add_all(x, axis):
+    pieces = lax.all_gather(x, axis)
+    return jnp.sum(pieces, axis=0)
 
 
 def shifted(block, axis, distance):
@@ -138,7 +143,7 @@
     bin_of = jnp.sum(jnp.where(seg_match, reward_bins[0][None, :], 0), axis=1)
     bin_match = bin_of[:, None] == jnp.arange(BINS, dtype=jnp.int32)[None, :]
     local_hist = jnp.sum(jnp.where(bin_match, kept[:, None], 0.0), axis=0)
-    histogram = lax.psum(local_hist, ("dp", "ctx"))
+    histogram = add_all(local_hist, ("dp", "ctx"))
     return (attended.reshape(1, row_count, q_width), histogram)
 
 

time: 379 us -> 926 us (2.44)
  the two profiles are of different devices: /device:TPU:1 before, /device:TPU:32 now
where the time goes in v1:
time: 926 us; the launch traced here: 924 us
  blocking collectives  671 us (72%)
  waiting for transfers between devices  113 us (12%)
  matrix products  69.7 us (8%)
  local copies, waits for them, and re-layouts  26.4 us (3%)
  other arithmetic  16.5 us (2%)
  between operations  14.3 us (2%)
  starting transfers between devices  12.5 us (1%)
    all_gather x1, blocking collectives, add_all(): pieces = lax.all_gather(x, axis)  623 us
    all_gather x1, waiting for transfers between devices, local(): value_rows = lax.all_gather(packed_values, 'ctx', axis=0, tiled=True)  84.1 us
    dot_general x16, matrix products, attend_block(): jnp.einsum('gjqk,kgd->qgjd', weights.astype(jnp.bfloat16), value_rows.res...  58.5 us
    all_gather x1, blocking collectives, local(): key_segments = lax.all_gather(seg_local, 'ctx', axis=0, tiled=True)  39.9 us
    all_gather x1, waiting for transfers between devices, local(): key_rows = lax.all_gather(packed_keys, 'ctx', axis=0, tiled=True)  23.6 us
  transfers between devices with their start and end apart: 5, of which 3 were waited for; matrix products, arithmetic and copies ran while one was open for 11% of the time, Pallas kernels for 0%

profile of v1, /device:TPU:32, one launch (start us, length us, event | category | flops | bytes accessed | tf_op | source)
XLA Modules:
  0.0 924.5 jit_solution(3292464791563668432)
XLA Ops:
  8.7 1.0 reshape_squeeze.9
  10.6 5.4 all-to-all-start
  17.6 4.9 all-to-all-done
  23.9 9.0 all_to_all.15
  35.1 1.5 copy.39
  36.6 3.7 all-to-all-start.1
  40.3 3.3 collective-permute-start
  43.6 39.9 %all-gather = s32[1,2048]{1,0:T(1,128)S(1)} all-gather(s32[1,128]{1,0:T(1,128)S(1)} %copy-done.3), channel_id=2, replica_groups=mesh['dp'=16,'ctx'=16] {'ctx'}, dimensions={1}, use_global_device_ids=true | all-gather | bytes 8704 | tf_op jit(solution)/shard_map/all_gather | solution.py:116
  85.7 23.6 %all-gather.6.cloned.1.call-done = bf16[2048,512]{0,1:T(8,128)(2,1)} async-done(((bf16[128,512]{0,1:T(8,128)(2,1)}), bf16[2048,512]{0,1:T(8,128)(2,1)}) %all-gather.6.cloned.1.call-update) | async-done | bytes 2097168 | tf_op jit(solution)/shard_map/all_gather | solution.py:114
  109.4 84.1 %all-gather.8.cloned.1.call-done = bf16[2048,512]{0,1:T(8,128)(2,1)} async-done(((bf16[128,512]{0,1:T(8,128)(2,1)}), bf16[2048,512]{0,1:T(8,128)(2,1)}) %all-gather.8.cloned.1.call-update) | async-done | bytes 2097168 | tf_op jit(solution)/shard_map/all_gather | solution.py:115
  193.4 96.3 %while.18 = (s32[]{:T(128)}, f32[4,8,128]{2,1,0:T(8,128)S(1)}, f32[4,8,128]{2,1,0:T(8,128)S(1)}, f32[128,4,8,128]{0,3,2,1:T(8,128)}, s32[1,128]{1,0:T(1,128)S(1)...) while((s32[]{:T(128)}, f32[4,8,128]{2,1,0:T(8,128)S(1)}, ...), condition=%wide.region_6.7_spmd.clone, body=%wide.region_3.6_spmd.clone.sunk | while | flops 276898048 | bytes 12652751 | solution.py:129
  193.6 1.0 constant_dynamic-slice_fusion.4
  195.2 2.2 bitcast_add_fusion.3
  198.2 1.0 constant_dynamic-slice_fusion.4
  199.7 3.7 bitcast_add_fusion.3
  204.3 1.0 constant_dynamic-slice_fusion.4
  205.8 3.8 bitcast_add_fusion.3
  210.4 1.0 constant_dynamic-slice_fusion.4
  211.9 3.8 bitcast_add_fusion.3
  216.5 1.0 constant_dynamic-slice_fusion.4
  218.1 3.8 bitcast_add_fusion.3
  222.6 1.0 constant_dynamic-slice_fusion.4
  224.2 3.8 bitcast_add_fusion.3
  228.8 1.0 constant_dynamic-slice_fusion.4
  230.3 3.8 bitcast_add_fusion.3
  234.9 1.0 constant_dynamic-slice_fusion.4
  236.4 3.8 bitcast_add_fusion.3
  241.0 1.0 constant_dynamic-slice_fusion.4
  242.6 3.8 bitcast_add_fusion.3
  247.1 1.0 constant_dynamic-slice_fusion.4
  248.7 3.8 bitcast_add_fusion.3
  253.2 1.0 constant_dynamic-slice_fusion.4
  254.8 3.8 bitcast_add_fusion.3
  259.4 1.0 constant_dynamic-slice_fusion.4
  260.9 3.8 bitcast_add_fusion.3
  265.5 1.0 constant_dynamic-slice_fusion.4
  267.0 3.8 bitcast_add_fusion.3
  271.6 1.0 constant_dynamic-slice_fusion.4
  273.2 3.8 bitcast_add_fusion.3
  277.7 1.0 constant_dynamic-slice_fusion.4
  279.3 3.8 bitcast_add_fusion.3
  283.9 1.0 constant_dynamic-slice_fusion.4
  285.4 3.8 bitcast_add_fusion.3
  289.8 1.9 divide_convert_fusion
  291.6 1.3 copy.34
  293.0 1.1 compare_select_fusion
  294.2 622.5 %all-gather.2 = f32[256,1,512]{2,1,0:T(1,128)S(1)} all-gather(f32[1,1,512]{2,1,0:T(1,128)S(1)} %bitcast.113), channel_id=3, replica_groups=mesh['dp'=16,'ctx'=16] {'dp','ctx'}, dimensions={0}, use_global_device_ids=true | all-gather | bytes 526336 | tf_op jit(solution)/shard_map/all_gather | solution.py:17
  916.7 0.9 reduce_sum.75
  (176 shorter events, 30.4 us)
Async XLA Ops:
  7.2 285.8 %copy-start = (f32[4096]{0:T(1024)S(1)}, f32[4096]{0:T(1024)}, u32[]{:S(2)}) copy-start(f32[4096]{0:T(1024)} %param.15) | copy-start | bytes 49156
  7.2 16.4 %copy-start.2 = (bf16[1,128,512]{2,1,0:T(8,128)(2,1)S(1)}, bf16[1,128,512]{2,1,0:T(8,128)(2,1)}, u32[]{:S(2)}) copy-start(bf16[1,128,512]{2,1,0:T(8,128)(2,1)} %param.11) | copy-start | bytes 393220
  9.7 24.4 %copy-start.1 = (bf16[1,128,4096]{2,1,0:T(8,128)(2,1)S(1)}, bf16[1,128,4096]{2,1,0:T(8,128)(2,1)}, u32[]{:S(2)}) copy-start(bf16[1,128,4096]{2,1,0:T(8,128)(2,1)} %param.9) | copy-start | bytes 3145732
  10.6 11.9 %all-to-all-start = ((bf16[16,8,512]{2,1,0:T(8,128)(2,1)}), bf16[16,8,512]{2,1,0:T(8,128)(2,1)S(1)}, u32[]{:S(2)}, u32[]{:S(2)}) async-start(bf16[16,8,512]{2,1,0:T(8,128)(2,1)} %bitcast.29), calls=%async_computation | async-start | bytes 262144 | tf_op jit(solution)/shard_map/all_to_all | solution.py:61
  16.0 93.4 %all-gather.6.cloned.1.call-start = ((), (), s32[]{:S(2)}) async-start(), calls=%async_computation.3 | async-start | bytes 2228224 | tf_op jit(solution)/shard_map/all_gather | solution.py:114
  23.6 169.9 %all-gather.8.cloned.1.call-start = ((), (), s32[]{:S(2)}) async-start(), calls=%async_computation.4 | async-start | bytes 2228224 | tf_op jit(solution)/shard_map/all_gather | solution.py:115
  35.1 5.2 copy-start.3
  35.1 48.5 %copy-start.4 = (s32[1,16]{1,0:T(1,128)S(1)}, s32[1,16]{1,0:T(1,128)}, u32[]{:S(2)}) copy-start(s32[1,16]{1,0:T(1,128)} %param.14) | copy-start | bytes 196
  36.6 47.1 %all-to-all-start.1 = ((bf16[16,8,4096]{2,1,0:T(8,128)(2,1)}), bf16[16,8,4096]{2,1,0:T(8,128)(2,1)S(1)}, u32[]{:S(2)}, u32[]{:S(2)}) async-start(bf16[16,8,4096]{2,1,0:T(8,128)(2,1)} %bitcast.33), calls=%async_computation.1 | async-start | bytes 2097152 | tf_op jit(solution)/shard_map/all_to_all | solution.py:60
  40.3 252.6 %collective-permute-start = (s32[1]{0:T(128)}, s32[1]{0:T(128)}, u32[]{:S(2)}, u32[]{:S(2)}) collective-permute-start(s32[1]{0:T(128)} %bitcast.9), channel_id=1, source_target_pairs={{1,0},{2,1},{3,2},{4,3},{5,4},{6,5},{7,6},{8,7},{9,8},{10,9},{11,1... | collective-permute-start | bytes 20 | tf_op jit(solution)/shard_map/ppermute | solution.py:24
Sparse Core Ops, SparseCore 0:
  23.7 85.6 all-gather.5
  111.8 81.5 all-gather.7
